TPU v7x, 32 devices: a whole 2x2x4 slice. The times are simulated.
32 devices in a mesh: dp: 2 (over core), expert: 16 (over z, y, x).
Axes of the slice: x: 2, y: 2, z: 4, core: 2. Of those that a mesh axis runs over, the one named last changes fastest.
Arguments:
- tokens: bfloat16 [2048, 2048], P('expert'), may hold values from -6 to 6
- out_grad: bfloat16 [2048, 2048], P('expert'), may hold values from -6 to 6
- route_ids: int32 [2048, 8], P('expert'), may hold values from 0 to 15, all different within a row; in each aligned block of 128 rows (0 to 127, 128 to 255, ...) at most 72 rows name the same one
- route_probs: float32 [2048, 8], P('expert'), may hold values from 0.05 to 1
- gate_store: bfloat16 [16, 2048, 768], P(None, 'expert', 'dp'), may hold values from -0.125 to 0.125
- up_store: bfloat16 [16, 2048, 768], P(None, 'expert', 'dp'), may hold values from -0.125 to 0.125
- down_store: bfloat16 [16, 2048, 768], P(None, 'expert', 'dp'), may hold values from -0.21875 to 0.21875
Outputs:
- grad_gate: bfloat16 [16, 2048, 768], P('expert', None, 'dp')
- grad_up: bfloat16 [16, 2048, 768], P('expert', None, 'dp')
- grad_down: bfloat16 [16, 2048, 768], P('expert', None, 'dp')
- grad_tokens: bfloat16 [2048, 2048], P('expert')
Inputs may be any that keep to these rules, and one draw needn't show every extreme that they name: `route_ids`: among the 128 tokens of one device no expert is named more than 72 times, and in every draw some expert is named exactly 72 times by some device's tokens.
All inputs are finite; a program needn't handle non-finite values.
Results may differ from a plain program's by a relative error of at most 0.0065.
Values may be sent and summed in bfloat16 or wider, within the bound.
A program may use at most 128 MiB of HBM per device.

v0:
```python
import jax
import jax.numpy as jnp
from jax import lax
from jax.sharding import PartitionSpec as P


def on_device(tokens, out_grad, route_ids, route_probs, gate_store, up_store, down_store):
    tok_rows, model_width = tokens.shape
    top_count = route_ids.shape[1]
    experts = lax.axis_size("expert")
    capacity = max(2, 9 * tok_rows * top_count // (8 * experts))
    slot_total = tok_rows * top_count
    flat_ids = route_ids.reshape(-1)
    expert_range = jnp.arange(experts, dtype=jnp.int32)
    per_count = jnp.sum((flat_ids[:, None] == expert_range[None, :]).astype(jnp.int32), axis=0)
    offsets = jnp.cumsum(per_count) - per_count
    order = jnp.argsort(flat_ids, stable=True)
    sorted_ids = flat_ids[order]
    sorted_rank = jnp.arange(slot_total, dtype=jnp.int32) - offsets[sorted_ids]
    slot_rank = jnp.zeros((slot_total,), jnp.int32).at[order].set(sorted_rank)
    slot_place = flat_ids * capacity + slot_rank
    source = (
        jnp.full((experts * capacity,), slot_total, jnp.int32)
        .at[slot_place]
        .set(jnp.arange(slot_total, dtype=jnp.int32))
    )
    filled = source < slot_total
    safe_index = jnp.where(filled, source, 0)
    owner_row = safe_index // top_count
    x_slots = jnp.where(filled[:, None], tokens[owner_row], jnp.zeros((), jnp.bfloat16))
    slot_prob = jnp.where(filled, route_probs.reshape(-1)[safe_index], 0.0)
    dy_slots = (slot_prob[:, None] * out_grad[owner_row].astype(jnp.float32)).astype(jnp.bfloat16)
    x_slots = x_slots.reshape(experts, capacity, model_width)
    dy_slots = dy_slots.reshape(experts, capacity, model_width)
    gate_all, up_all, down_all = (
        lax.all_to_all(gate_store, "expert", split_axis=0, concat_axis=1, tiled=True),
        lax.all_to_all(up_store, "expert", split_axis=0, concat_axis=1, tiled=True),
        lax.all_to_all(down_store, "expert", split_axis=0, concat_axis=1, tiled=True),
    )
    gate_panel = gate_all[0]
    up_panel = up_all[0]
    col_width = model_width // lax.axis_size("dp")
    col_start = lax.axis_index("dp") * col_width
    x_part = lax.dynamic_slice_in_dim(x_slots, col_start, col_width, 2)
    dy_part = lax.dynamic_slice_in_dim(dy_slots, col_start, col_width, 2)
    x_sent, dy_sent = (
        lax.all_to_all(x_part, "expert", split_axis=0, concat_axis=0, tiled=True),
        lax.all_to_all(dy_part, "expert", split_axis=0, concat_axis=0, tiled=True),
    )
    x_in, dy_in = (
        lax.all_gather(x_sent, "dp", axis=2, tiled=True),
        lax.all_gather(dy_sent, "dp", axis=2, tiled=True),
    )
    rows_in = x_in.reshape(-1, model_width)
    dy_rows = dy_in.reshape(-1, model_width)
    gate_pre = jnp.dot(rows_in, gate_panel, preferred_element_type=jnp.float32)
    up_pre = jnp.dot(rows_in, up_panel, preferred_element_type=jnp.float32)
    sigmoid_gate = jax.nn.sigmoid(gate_pre)
    activation = (gate_pre * sigmoid_gate * up_pre).astype(jnp.bfloat16)
    down_panel = down_all[0]
    act_grad = jnp.dot(dy_rows, down_panel, preferred_element_type=jnp.float32)
    up_grad = (act_grad * gate_pre * sigmoid_gate).astype(jnp.bfloat16)
    gate_grad = (act_grad * up_pre * sigmoid_gate * (1.0 + gate_pre * (1.0 - sigmoid_gate))).astype(
        jnp.bfloat16
    )
    contract = (((0,), (0,)), ((), ()))
    grad_down = lax.dot_general(
        dy_rows, activation, contract, preferred_element_type=jnp.float32
    ).astype(jnp.bfloat16)
    grad_gate = lax.dot_general(
        rows_in, gate_grad, contract, preferred_element_type=jnp.float32
    ).astype(jnp.bfloat16)
    grad_up = lax.dot_general(
        rows_in, up_grad, contract, preferred_element_type=jnp.float32
    ).astype(jnp.bfloat16)
    back_contract = (((1,), (1,)), ((), ()))
    slot_half = lax.dot_general(
        gate_grad, gate_panel, back_contract, preferred_element_type=jnp.float32
    ) + lax.dot_general(up_grad, up_panel, back_contract, preferred_element_type=jnp.float32)
    summed = lax.psum_scatter(
        slot_half.reshape(experts, capacity, model_width), "dp", scatter_dimension=2, tiled=True
    )
    returned = lax.all_to_all(
        summed.astype(jnp.bfloat16), "expert", split_axis=0, concat_axis=0, tiled=True
    )
    share_width = returned.shape[2]
    slot_values = returned.reshape(experts * capacity, share_width)[slot_place]
    token_share = jnp.sum(
        slot_values.reshape(tok_rows, top_count, share_width).astype(jnp.float32), axis=1
    ).astype(jnp.bfloat16)
    grad_tokens = lax.all_gather(token_share, "dp", axis=1, tiled=True)
    return (grad_gate[None], grad_up[None], grad_down[None], grad_tokens)


def gathered(tokens, out_grad, route_ids, route_probs, gate_store, up_store, down_store):
    tok_rows, model_width = tokens.shape
    experts = lax.axis_size("expert")
    half = tok_rows // lax.axis_size("dp")
    start = lax.axis_index("dp") * half
    both = ("expert", "dp")
    chosen = route_ids[:, :, None] == jnp.arange(experts, dtype=jnp.int32)[None, None, :]
    weight = jnp.sum(jnp.where(chosen, route_probs[:, :, None], 0.0), axis=1)
    weight = lax.all_to_all(
        weight.T.reshape(experts, tok_rows), "expert", split_axis=0, concat_axis=0, tiled=True
    )
    weight = weight.reshape(-1, 1)
    x_all = lax.all_gather(
        lax.dynamic_slice_in_dim(tokens, start, half, 0), both, axis=0, tiled=True
    )
    g_all = lax.all_gather(
        lax.dynamic_slice_in_dim(out_grad, start, half, 0), both, axis=0, tiled=True
    )
    gate_panel, up_panel, down_panel = (
        lax.all_to_all(store, "expert", split_axis=0, concat_axis=1, tiled=True)[0]
        for store in (gate_store, up_store, down_store)
    )
    gate_pre = jnp.dot(x_all, gate_panel, preferred_element_type=jnp.float32)
    up_pre = jnp.dot(x_all, up_panel, preferred_element_type=jnp.float32)
    act_grad = jnp.dot(g_all, down_panel, preferred_element_type=jnp.float32) * weight
    sig = jax.nn.sigmoid(gate_pre)
    activation = (gate_pre * sig * up_pre * weight).astype(jnp.bfloat16)
    up_grad = (act_grad * gate_pre * sig).astype(jnp.bfloat16)
    gate_grad = (act_grad * up_pre * sig * (1.0 + gate_pre * (1.0 - sig))).astype(jnp.bfloat16)
    back = (((1,), (1,)), ((), ()))
    slot_half = lax.dot_general(
        gate_grad, gate_panel, back, preferred_element_type=jnp.float32
    ) + lax.dot_general(up_grad, up_panel, back, preferred_element_type=jnp.float32)
    share = lax.psum_scatter(slot_half.astype(jnp.bfloat16), both, scatter_dimension=0, tiled=True)
    grad_tokens = lax.all_gather(share, "dp", axis=0, tiled=True)
    outer = (((0,), (0,)), ((), ()))
    grad_down = lax.dot_general(
        g_all, activation, outer, preferred_element_type=jnp.float32
    ).astype(jnp.bfloat16)
    grad_gate = lax.dot_general(x_all, gate_grad, outer, preferred_element_type=jnp.float32).astype(
        jnp.bfloat16
    )
    grad_up = lax.dot_general(x_all, up_grad, outer, preferred_element_type=jnp.float32).astype(
        jnp.bfloat16
    )
    return (grad_gate[None], grad_up[None], grad_down[None], grad_tokens)


def choose(tokens, out_grad, route_ids, *rest):
    if lax.axis_size("expert") <= 2 * route_ids.shape[1]:
        return gathered(tokens, out_grad, route_ids, *rest)
    return on_device(tokens, out_grad, route_ids, *rest)


def solution(mesh):
    return jax.shard_map(
        choose,
        mesh=mesh,
        in_specs=(
            P("expert", None),
            P("expert", None),
            P("expert", None),
            P("expert", None),
            P(None, "expert", "dp"),
            P(None, "expert", "dp"),
            P(None, "expert", "dp"),
        ),
        out_specs=(
            P("expert", None, "dp"),
            P("expert", None, "dp"),
            P("expert", None, "dp"),
            P("expert", None),
        ),
        check_vma=False,
    )
```

profile of v0, /device:TPU:0, one launch (start us, length us, event | category | flops | bytes accessed | tf_op | source)
XLA Modules:
  0.0 414.2 jit_solution(4239823326702032732)
XLA Ops:
  7.2 1.0 copy-done
  8.2 0.7 constant_dynamic-slice_fusion.1
  9.0 0.0 all-gather.5.cloned.1.call-start
  9.0 1.7 constant_dynamic-slice_fusion
  10.7 0.8 select_reduce_fusion
  11.6 15.4 %all_to_all.36 = f32[16,1,128]{2,1,0:T(1,128)S(1)} all-to-all(f32[16,1,128]{2,1,0:T(1,128)S(1)} %bitcast.34), channel_id=1, replica_groups=mesh['dp'=2,'expert'=16] {'expert'}, dimensions={0} | all-to-all | bytes 16384 | tf_op jit(solution)/shard_map/all_to_all | solution.py:103
  27.0 52.7 %all_to_all.37 = bf16[16,128,384]{2,1,0:T(8,128)(2,1)} all-to-all(bf16[16,128,384]{2,1,0:T(8,128)(2,1)} %param.11), channel_id=1, replica_groups=mesh['dp'=2,'expert'=16] {'expert'}, dimensions={0} | all-to-all | bytes 3145728 | tf_op jit(solution)/shard_map/all_to_all | solution.py:114
  79.7 56.4 %all_to_all.38 = bf16[16,128,384]{2,1,0:T(8,128)(2,1)S(1)} all-to-all(bf16[16,128,384]{2,1,0:T(8,128)(2,1)S(1)} %copy-done.7), channel_id=1, replica_groups=mesh['dp'=2,'expert'=16] {'expert'}, dimensions={0} | all-to-all | bytes 3145728 | tf_op jit(solution)/shard_map/all_to_all | solution.py:114
  136.1 4.6 %all-to-all-start = ((bf16[16,128,384]{2,1,0:T(8,128)(2,1)}), bf16[16,128,384]{2,1,0:T(8,128)(2,1)}, u32[]{:S(2)}, u32[]{:S(2)}) async-start(bf16[16,128,384]{2,1,0:T(8,128)(2,1)} %param.13), calls=%async_computation | async-start | bytes 3145728 | tf_op jit(solution)/shard_map/all_to_all | solution.py:114
  140.7 0.0 reduce-scatter.2.cloned.1.call-start
  140.8 10.2 %fusion.7 = f32[2048,384]{1,0:T(8,128)} fusion(bf16[2048,2048]{1,0:T(8,128)(2,1)} %all-gather.3.cloned.1.call-done, bf16[2048,384]{1,0:T(8,128)(2,1)} %bitcast.32), kind=kOutput, calls=%fused_computation.20 | convolution fusion | flops 3221225472 | bytes 13107200 | tf_op jit(solution)/shard_map/dot_general | solution.py:117
  151.0 6.4 %fusion.6 = f32[2048,384]{1,0:T(8,128)} fusion(bf16[2048,2048]{1,0:T(8,128)(2,1)S(1)} %copy-done.8, bf16[2048,384]{1,0:T(8,128)(2,1)S(1)} %bitcast.30), kind=kOutput, calls=%fused_computation.19 | convolution fusion | flops 3221225472 | bytes 13107200 | tf_op jit(solution)/shard_map/dot_general | solution.py:118
  157.3 30.6 %all-to-all-done = bf16[16,128,384]{2,1,0:T(8,128)(2,1)} async-done(((bf16[16,128,384]{2,1,0:T(8,128)(2,1)}), bf16[16,128,384]{2,1,0:T(8,128)(2,1)}, u32[]{:S(2)}, u32[]{:S(2)}) %all-to-all-start) | async-done | bytes 1572896 | tf_op jit(solution)/shard_map/all_to_all | solution.py:114
  187.9 37.2 %all-gather.5.cloned.1.call-done = bf16[2048,2048]{1,0:T(8,128)(2,1)} async-done(((bf16[64,2048]{1,0:T(8,128)(2,1)}), bf16[2048,2048]{1,0:T(8,128)(2,1)}) %all-gather.5.cloned.1.call-update) | async-done | bytes 8388624 | tf_op jit(solution)/shard_map/all_gather | solution.py:110
  225.1 11.5 %multiply_convert_fusion.1 = (bf16[2048,384]{1,0:T(8,128)(2,1)S(1)}, bf16[2048,384]{1,0:T(8,128)(2,1)S(1)}) fusion(f32[2048,384]{1,0:T(8,128)} %fusion.7, f32[2048,384]{1,0:T(8,128)} %fusion.6, f32[2048]{0:T(1024)S(1)} %bitcast.35, bf16[2048,2048]{1,0:T(8,128)(2,1)} %all-gather.5.cloned.1.call-done, bf16[2048,384]{1,0:T(8,128)(2,1)} %bitcast), kind=kOutput, calls=%fused_computation.2 | convolution fusion | flops 3232235520 | bytes 19406848 | tf_op jit(solution)/shard_map/dot_general | solution.py:119
  236.7 8.2 %fusion.8 = f32[2048,2048]{1,0:T(8,128)} fusion(bf16[2048,384]{1,0:T(8,128)(2,1)S(1)} %get-tuple-element.5, bf16[2048,384]{1,0:T(8,128)(2,1)S(1)} %bitcast.33), kind=kOutput, calls=%fused_computation.21 | convolution fusion | flops 3221225472 | bytes 19922944 | tf_op jit(solution)/shard_map/dot_general | solution.py:125
  244.9 10.3 %add_convert_fusion = bf16[2048,2048]{1,0:T(8,128)(2,1)} fusion(f32[2048,2048]{1,0:T(8,128)} %fusion.8, bf16[2048,384]{1,0:T(8,128)(2,1)S(1)} %get-tuple-element.4, bf16[2048,384]{1,0:T(8,128)(2,1)S(1)} %bitcast.31), kind=kOutput, calls=%fused_computation | convolution fusion | flops 3229614080 | bytes 28311552 | tf_op jit(solution)/shard_map/dot_general | solution.py:127
  255.2 1.4 copy-done.6
  256.6 9.3 %fusion.1 = bf16[1,2048,384]{2,1,0:T(8,128)(2,1)} fusion(bf16[2048,2048]{1,0:T(8,128)(2,1)} %all-gather.3.cloned.1.call-done, bf16[2048,384]{1,0:T(8,128)(2,1)S(1)} %copy-done.6), kind=kOutput, calls=%fused_computation.10 | convolution fusion | flops 3222011904 | bytes 11534336 | tf_op jit(solution)/shard_map/dot_general | solution.py:137
  266.0 9.4 %fusion = bf16[1,2048,384]{2,1,0:T(8,128)(2,1)} fusion(bf16[2048,2048]{1,0:T(8,128)(2,1)} %all-gather.3.cloned.1.call-done, bf16[2048,384]{1,0:T(8,128)(2,1)S(1)} %copy-done.4), kind=kOutput, calls=%fused_computation.9 | convolution fusion | flops 3222011904 | bytes 11534336 | tf_op jit(solution)/shard_map/dot_general | solution.py:134
  275.4 6.0 %fusion.2 = bf16[1,2048,384]{2,1,0:T(8,128)(2,1)} fusion(bf16[2048,2048]{1,0:T(8,128)(2,1)S(1)} %bitcast.38, f32[2048,384]{1,0:T(8,128)S(1)} %copy-done.10, f32[2048,384]{1,0:T(8,128)S(1)} %copy-done.9, f32[2048]{0:T(1024)S(1)} %bitcast.36), kind=kOutput, calls=%fused_computation.11 | convolution fusion | flops 3227516928 | bytes 16261120 | tf_op jit(solution)/shard_map/dot_general | solution.py:131
  281.4 123.1 %reduce-scatter.2.cloned.1.call-done = bf16[64,2048]{1,0:T(8,128)(2,1)} async-done(((bf16[2048,2048]{1,0:T(8,128)(2,1)}), bf16[64,2048]{1,0:T(8,128)(2,1)}) %reduce-scatter.2.cloned.1.call-update) | async-done | bytes 262160 | tf_op jit(solution)/shard_map/reduce_scatter | solution.py:128
  404.5 2.4 all_gather.11
  406.8 0.8 copy.19
  (30 shorter events, 0.2 us)
Async XLA Ops:
  7.2 1.1 copy-start
  7.2 133.6 %all-gather.3.cloned.1.call-start = ((), (), s32[]{:S(2)}) async-start(), calls=%async_computation.5 | async-start | bytes 8650752 | tf_op jit(solution)/shard_map/all_gather | solution.py:107
  9.0 216.2 %all-gather.5.cloned.1.call-start = ((), (), s32[]{:S(2)}) async-start(), calls=%async_computation.6 | async-start | bytes 8650752 | tf_op jit(solution)/shard_map/all_gather | solution.py:110
  10.7 69.0 %copy-start.7 = (bf16[16,128,384]{2,1,0:T(8,128)(2,1)S(1)}, bf16[16,128,384]{2,1,0:T(8,128)(2,1)}, u32[]{:S(2)}) copy-start(bf16[16,128,384]{2,1,0:T(8,128)(2,1)} %param.12) | copy-start | bytes 4718596
  136.1 51.8 %all-to-all-start = ((bf16[16,128,384]{2,1,0:T(8,128)(2,1)}), bf16[16,128,384]{2,1,0:T(8,128)(2,1)}, u32[]{:S(2)}, u32[]{:S(2)}) async-start(bf16[16,128,384]{2,1,0:T(8,128)(2,1)} %param.13), calls=%async_computation | async-start | bytes 3145728 | tf_op jit(solution)/shard_map/all_to_all | solution.py:114
  140.7 263.7 %reduce-scatter.2.cloned.1.call-start = ((), (), s32[]{:S(2)}) async-start(), calls=%async_computation.7 | async-start | bytes 8650752 | tf_op jit(solution)/shard_map/reduce_scatter | solution.py:128
  140.8 10.2 %copy-start.8 = (bf16[2048,2048]{1,0:T(8,128)(2,1)S(1)}, bf16[2048,2048]{1,0:T(8,128)(2,1)}, u32[]{:S(2)}) copy-start(bf16[2048,2048]{1,0:T(8,128)(2,1)} %all-gather.3.cloned.1.call-done) | copy-start | bytes 25165828
  225.1 11.6 %copy-start.2 = (bf16[16,128,384]{2,1,0:T(8,128)(2,1)S(1)}, bf16[16,128,384]{2,1,0:T(8,128)(2,1)}, u32[]{:S(2)}) copy-start(bf16[16,128,384]{2,1,0:T(8,128)(2,1)} %all_to_all.37) | copy-start | bytes 4718596
  236.7 8.2 %copy-start.3 = (bf16[2048,384]{1,0:T(8,128)(2,1)}, bf16[2048,384]{1,0:T(8,128)(2,1)S(1)}, u32[]{:S(2)}) copy-start(bf16[2048,384]{1,0:T(8,128)(2,1)S(1)} %get-tuple-element.5) | copy-start | bytes 4718596
  236.7 8.2 %copy-start.5 = (bf16[2048,384]{1,0:T(8,128)(2,1)}, bf16[2048,384]{1,0:T(8,128)(2,1)S(1)}, u32[]{:S(2)}) copy-start(bf16[2048,384]{1,0:T(8,128)(2,1)S(1)} %get-tuple-element.4) | copy-start | bytes 4718596
  255.2 1.4 copy-start.6
  256.6 9.3 %copy-start.4 = (bf16[2048,384]{1,0:T(8,128)(2,1)S(1)}, bf16[2048,384]{1,0:T(8,128)(2,1)}, u32[]{:S(2)}) copy-start(bf16[2048,384]{1,0:T(8,128)(2,1)} %copy-done.3) | copy-start | bytes 4718596
  256.6 18.7 %slice-start = ((s8[8388608]{0:T(1024)(128)(4,1)}), s8[4194304]{0:T(1024)(128)(4,1)S(1)}, s32[]{:S(2)}) async-start(s8[8388608]{0:T(1024)(128)(4,1)} %bitcast.37), calls=%async_computation.8 | async-start | bytes 8388608
  266.0 9.4 %slice-start.1 = ((s8[8388608]{0:T(1024)(128)(4,1)}), s8[4194304]{0:T(1024)(128)(4,1)S(1)}, s32[]{:S(2)}) async-start(s8[8388608]{0:T(1024)(128)(4,1)} %bitcast.37), calls=%async_computation.9 | async-start | bytes 8388608
  266.0 9.4 %copy-start.9 = (f32[2048,384]{1,0:T(8,128)S(1)}, f32[2048,384]{1,0:T(8,128)}, u32[]{:S(2)}) copy-start(f32[2048,384]{1,0:T(8,128)} %fusion.7) | copy-start | bytes 9437188
  266.0 9.4 %copy-start.10 = (f32[2048,384]{1,0:T(8,128)S(1)}, f32[2048,384]{1,0:T(8,128)}, u32[]{:S(2)}) copy-start(f32[2048,384]{1,0:T(8,128)} %fusion.6) | copy-start | bytes 9437188
  275.4 132.3 %copy-start.1 = (bf16[128,2048]{1,0:T(8,128)(2,1)S(1)}, bf16[128,2048]{1,0:T(8,128)(2,1)}, u32[]{:S(2)}) copy-start(bf16[128,2048]{1,0:T(8,128)(2,1)} %param.7) | copy-start | bytes 1572868
Sparse Core Ops, SparseCore 0:
  11.4 115.0 all-gather.2
  130.0 95.1 all-gather.4
  255.4 149.0 reduce-scatter.1
where the time goes:
time: 415 us; the launch traced here: 414 us
  waiting for transfers between devices  191 us (46%)
  blocking collectives  127 us (31%)
  matrix products  71.2 us (17%)
  between operations  13.9 us (3%)
  local copies, waits for them, and re-layouts  5.61 us (1%)
  starting transfers between devices  4.7 us (1%)
    reduce_scatter x1, waiting for transfers between devices, gathered(): lax.psum_scatter(slot_half.astype(jnp.bfloat16), both, scatter_dimension=...  123 us
    all_to_all x2, blocking collectives, gathered(): lax.all_to_all(store, 'expert', split_axis=0, concat_axis=1, tiled=True)[0]  109 us
    all_gather x1, waiting for transfers between devices, gathered(): lax.all_gather(lax.dynamic_slice_in_dim(out_grad, start, half, 0), both,...  37.2 us
    all_to_all x1, waiting for transfers between devices, gathered(): lax.all_to_all(store, 'expert', split_axis=0, concat_axis=1, tiled=True)[0]  30.6 us
    all_to_all x1, blocking collectives, gathered(): lax.all_to_all(weight.T.reshape(experts, tok_rows), 'expert', split_axis=...  15.4 us
    dot_general x1, matrix products, gathered(): jnp.dot(g_all, down_panel, preferred_element_type=jnp.float32) * weight  11.5 us
    dot_general x1, matrix products, gathered(): lax.dot_general(up_grad, up_panel, back, preferred_element_type=jnp.float32)  10.3 us
    dot_general x1, matrix products, gathered(): gate_pre = jnp.dot(x_all, gate_panel, preferred_element_type=jnp.float32)  10.2 us
  transfers between devices with their start and end apart: 4, of which 3 were waited for; matrix products, arithmetic and copies ran while one was open for 11% of the time, Pallas kernels for 0%

commit v1 on v0

--- a/solution.py
+++ b/solution.py
@@ -107,8 +107,14 @@
     x_all = lax.all_gather(
         lax.dynamic_slice_in_dim(tokens, start, half, 0), both, axis=0, tiled=True
     )
-    g_all = lax.all_gather(
-        lax.dynamic_slice_in_dim(out_grad, start, half, 0), both, axis=0, tiled=True
+    g_all = jnp.concatenate(
+        lax.all_to_all(
+            jnp.stack([lax.dynamic_slice_in_dim(out_grad, start, half, 0)] * lax.axis_size(both)),
+            both,
+            0,
+            0,
+        ),
+        axis=0,
     )
     gate_panel, up_panel, down_panel = (
         lax.all_to_all(store, "expert", split_axis=0, concat_axis=1, tiled=True)[0]

time: 415 us -> 558 us (1.34)
  waiting for transfers between devices: 191 us -> 348 us
  blocking collectives: 127 us -> 99.1 us
  starting transfers between devices: 4.7 us -> 14.1 us
    all_to_all x0 -> x1, waiting for transfers between devices: none -> 107 us  [gathered(): lax.all_to_all(jnp.stack([lax.dynamic_slice_in_dim(out_grad, start, half,...]
    all_gather x1, waiting for transfers between devices: 0.02 us -> 83.7 us  [gathered(): lax.all_gather(lax.dynamic_slice_in_dim(tokens, start, half, 0), both, ax...]
    all_gather x1 -> x0, waiting for transfers between devices: 37.2 us -> none  [gathered(): lax.all_gather(lax.dynamic_slice_in_dim(out_grad, start, half, 0), both,...]
    all_to_all x2, blocking collectives: 109 us -> 81.2 us  [gathered(): lax.all_to_all(store, 'expert', split_axis=0, concat_axis=1, tiled=True)[0]]
    all_to_all x0 -> x1, starting transfers between devices: none -> 9.63 us  [gathered(): lax.all_to_all(jnp.stack([lax.dynamic_slice_in_dim(out_grad, start, half,...]
    all_to_all x1, waiting for transfers between devices: 30.6 us -> 37.6 us  [gathered(): lax.all_to_all(store, 'expert', split_axis=0, concat_axis=1, tiled=True)[0]]
  transfers between devices with their start and end apart: 4 -> 4, of which waited for: 3 -> 4; matrix products, arithmetic and copies ran while one was open for 11% -> 9% of each run, Pallas kernels for 0% -> 0%
where the time goes in v1:
time: 558 us; the launch traced here: 557 us
  waiting for transfers between devices  348 us (62%)
  blocking collectives  99.1 us (18%)
  matrix products  75.3 us (13%)
  between operations  14.2 us (3%)
  starting transfers between devices  14.1 us (3%)
  local copies, waits for them, and re-layouts  5.9 us (1%)
    reduce_scatter x1, waiting for transfers between devices, gathered(): lax.psum_scatter(slot_half.astype(jnp.bfloat16), both, scatter_dimension=...  119 us
    all_to_all x1, waiting for transfers between devices, gathered(): lax.all_to_all(jnp.stack([lax.dynamic_slice_in_dim(out_grad, start, half,...  107 us
    all_gather x1, waiting for transfers between devices, gathered(): lax.all_gather(lax.dynamic_slice_in_dim(tokens, start, half, 0), both, ax...  83.7 us
    all_to_all x2, blocking collectives, gathered(): lax.all_to_all(store, 'expert', split_axis=0, concat_axis=1, tiled=True)[0]  81.2 us
    all_to_all x1, waiting for transfers between devices, gathered(): lax.all_to_all(store, 'expert', split_axis=0, concat_axis=1, tiled=True)[0]  37.6 us
    all_to_all x1, blocking collectives, gathered(): lax.all_to_all(weight.T.reshape(experts, tok_rows), 'expert', split_axis=...  15.4 us
    dot_general x1, matrix products, gathered(): jnp.dot(g_all, down_panel, preferred_element_type=jnp.float32) * weight  11.5 us
  transfers between devices with their start and end apart: 4, of which 4 were waited for; matrix products, arithmetic and copies ran while one was open for 9% of the time, Pallas kernels for 0%

profile of v1, /device:TPU:0, one launch (start us, length us, event | category | flops | bytes accessed | tf_op | source)
XLA Modules:
  0.0 557.4 jit_solution(6860681386524480749)
XLA Ops:
  7.2 0.9 select_reduce_fusion
  8.1 15.4 %all_to_all.41 = f32[16,1,128]{2,1,0:T(1,128)S(1)} all-to-all(f32[16,1,128]{2,1,0:T(1,128)S(1)} %bitcast.35), channel_id=1, replica_groups=mesh['dp'=2,'expert'=16] {'expert'}, dimensions={0} | all-to-all | bytes 16384 | tf_op jit(solution)/shard_map/all_to_all | solution.py:103
  23.5 40.9 %all_to_all.42 = bf16[16,128,384]{2,1,0:T(8,128)(2,1)} all-to-all(bf16[16,128,384]{2,1,0:T(8,128)(2,1)} %param.11), channel_id=1, replica_groups=mesh['dp'=2,'expert'=16] {'expert'}, dimensions={0} | all-to-all | bytes 3145728 | tf_op jit(solution)/shard_map/all_to_all | solution.py:120
  64.4 40.4 %all_to_all.43 = bf16[16,128,384]{2,1,0:T(8,128)(2,1)S(1)} all-to-all(bf16[16,128,384]{2,1,0:T(8,128)(2,1)S(1)} %copy-done.6), channel_id=1, replica_groups=mesh['dp'=2,'expert'=16] {'expert'}, dimensions={0} | all-to-all | bytes 3145728 | tf_op jit(solution)/shard_map/all_to_all | solution.py:120
  104.7 4.4 all-to-all-start.1
  109.2 0.0 all-gather.2.cloned.1.call-start
  109.2 0.7 constant_dynamic-slice_fusion.1
  110.0 37.6 %all-to-all-done.1 = bf16[16,128,384]{2,1,0:T(8,128)(2,1)} async-done(((bf16[16,128,384]{2,1,0:T(8,128)(2,1)}), bf16[16,128,384]{2,1,0:T(8,128)(2,1)}, u32[]{:S(2)}, u32[]{:S(2)}) %all-to-all-start.1) | async-done | bytes 1572896 | tf_op jit(solution)/shard_map/all_to_all | solution.py:120
  147.6 4.3 stack.2
  151.9 9.6 %all-to-all-start = ((bf16[32,64,2048]{2,1,0:T(8,128)(2,1)}), bf16[32,64,2048]{2,1,0:T(8,128)(2,1)}, u32[]{:S(2)}, u32[]{:S(2)}) async-start(bf16[32,64,2048]{2,1,0:T(8,128)(2,1)} %stack.2), calls=%async_computation | async-start | bytes 16777216 | tf_op jit(solution)/shard_map/all_to_all | solution.py:111
  161.5 0.0 reduce-scatter.2.cloned.1.call-start
  161.6 83.7 %all-gather.2.cloned.1.call-done = bf16[2048,2048]{1,0:T(8,128)(2,1)} async-done(((bf16[64,2048]{1,0:T(8,128)(2,1)}), bf16[2048,2048]{1,0:T(8,128)(2,1)}) %all-gather.2.cloned.1.call-update) | async-done | bytes 8388624 | tf_op jit(solution)/shard_map/all_gather | solution.py:107
  245.3 10.1 %fusion.7 = f32[2048,384]{1,0:T(8,128)} fusion(bf16[2048,2048]{1,0:T(8,128)(2,1)} %all-gather.2.cloned.1.call-done, bf16[2048,384]{1,0:T(8,128)(2,1)} %bitcast.33), kind=kOutput, calls=%fused_computation.20 | convolution fusion | flops 3221225472 | bytes 13107200 | tf_op jit(solution)/shard_map/dot_general | solution.py:123
  255.5 6.4 %fusion.6 = f32[2048,384]{1,0:T(8,128)} fusion(bf16[2048,2048]{1,0:T(8,128)(2,1)S(1)} %copy-done.8, bf16[2048,384]{1,0:T(8,128)(2,1)S(1)} %bitcast.31), kind=kOutput, calls=%fused_computation.19 | convolution fusion | flops 3221225472 | bytes 13107200 | tf_op jit(solution)/shard_map/dot_general | solution.py:124
  261.8 107.5 %all-to-all-done = bf16[32,64,2048]{2,1,0:T(8,128)(2,1)} async-done(((bf16[32,64,2048]{2,1,0:T(8,128)(2,1)}), bf16[32,64,2048]{2,1,0:T(8,128)(2,1)}, u32[]{:S(2)}, u32[]{:S(2)}) %all-to-all-start) | async-done | bytes 8388640 | tf_op jit(solution)/shard_map/all_to_all | solution.py:111
  369.3 11.5 %multiply_convert_fusion.1 = (bf16[2048,384]{1,0:T(8,128)(2,1)S(1)}, bf16[2048,384]{1,0:T(8,128)(2,1)S(1)}) fusion(f32[2048,384]{1,0:T(8,128)} %fusion.7, f32[2048,384]{1,0:T(8,128)} %fusion.6, f32[2048]{0:T(1024)S(1)} %bitcast.36, bf16[2048,2048]{1,0:T(8,128)(2,1)} %bitcast, bf16[2048,384]{1,0:T(8,128)(2,1)} %bitcast.1), kind=kOutput, calls=%fused_computation.2 | convolution fusion | flops 3232235520 | bytes 19406848 | tf_op jit(solution)/shard_map/dot_general | solution.py:125
  380.9 8.3 %fusion.8 = f32[2048,2048]{1,0:T(8,128)} fusion(bf16[2048,384]{1,0:T(8,128)(2,1)S(1)} %get-tuple-element.5, bf16[2048,384]{1,0:T(8,128)(2,1)S(1)} %bitcast.34), kind=kOutput, calls=%fused_computation.21 | convolution fusion | flops 3221225472 | bytes 19922944 | tf_op jit(solution)/shard_map/dot_general | solution.py:131
  389.2 10.3 %add_convert_fusion = bf16[2048,2048]{1,0:T(8,128)(2,1)} fusion(f32[2048,2048]{1,0:T(8,128)} %fusion.8, bf16[2048,384]{1,0:T(8,128)(2,1)S(1)} %get-tuple-element.4, bf16[2048,384]{1,0:T(8,128)(2,1)S(1)} %bitcast.32), kind=kOutput, calls=%fused_computation | convolution fusion | flops 3229614080 | bytes 28311552 | tf_op jit(solution)/shard_map/dot_general | solution.py:133
  399.5 9.6 %fusion = bf16[1,2048,384]{2,1,0:T(8,128)(2,1)} fusion(bf16[2048,2048]{1,0:T(8,128)(2,1)} %all-gather.2.cloned.1.call-done, bf16[2048,384]{1,0:T(8,128)(2,1)} %copy-done.5), kind=kOutput, calls=%fused_computation.9 | convolution fusion | flops 3222011904 | bytes 11534336 | tf_op jit(solution)/shard_map/dot_general | solution.py:140
  409.2 9.3 %fusion.1 = bf16[1,2048,384]{2,1,0:T(8,128)(2,1)} fusion(bf16[2048,2048]{1,0:T(8,128)(2,1)} %all-gather.2.cloned.1.call-done, bf16[2048,384]{1,0:T(8,128)(2,1)S(1)} %copy-done.4), kind=kOutput, calls=%fused_computation.10 | convolution fusion | flops 3222011904 | bytes 11534336 | tf_op jit(solution)/shard_map/dot_general | solution.py:143
  418.5 9.6 %fusion.2 = bf16[1,2048,384]{2,1,0:T(8,128)(2,1)} fusion(bf16[2048,2048]{1,0:T(8,128)(2,1)} %bitcast, f32[2048,384]{1,0:T(8,128)S(1)} %copy-done.10, f32[2048,384]{1,0:T(8,128)S(1)} %copy-done.9, f32[2048]{0:T(1024)S(1)} %bitcast.37), kind=kOutput, calls=%fused_computation.11 | convolution fusion | flops 3227516928 | bytes 16261120 | tf_op jit(solution)/shard_map/dot_general | solution.py:137
  428.2 119.3 %reduce-scatter.2.cloned.1.call-done = bf16[64,2048]{1,0:T(8,128)(2,1)} async-done(((bf16[2048,2048]{1,0:T(8,128)(2,1)}), bf16[64,2048]{1,0:T(8,128)(2,1)}) %reduce-scatter.2.cloned.1.call-update) | async-done | bytes 262160 | tf_op jit(solution)/shard_map/reduce_scatter | solution.py:134
  547.4 2.4 all_gather.7
  549.8 0.8 copy.19
  (25 shorter events, 0.1 us)
Async XLA Ops:
  7.2 102.1 %copy-start = (bf16[128,2048]{1,0:T(8,128)(2,1)S(1)}, bf16[128,2048]{1,0:T(8,128)(2,1)}, u32[]{:S(2)}) copy-start(bf16[128,2048]{1,0:T(8,128)(2,1)} %param.7) | copy-start | bytes 1572868
  7.2 57.2 %copy-start.6 = (bf16[16,128,384]{2,1,0:T(8,128)(2,1)S(1)}, bf16[16,128,384]{2,1,0:T(8,128)(2,1)}, u32[]{:S(2)}) copy-start(bf16[16,128,384]{2,1,0:T(8,128)(2,1)} %param.12) | copy-start | bytes 4718596
  64.4 45.6 %copy-start.7 = (bf16[128,2048]{1,0:T(8,128)(2,1)S(1)}, bf16[128,2048]{1,0:T(8,128)(2,1)}, u32[]{:S(2)}) copy-start(bf16[128,2048]{1,0:T(8,128)(2,1)} %param.8) | copy-start | bytes 1572868
  104.7 42.9 %all-to-all-start.1 = ((bf16[16,128,384]{2,1,0:T(8,128)(2,1)}), bf16[16,128,384]{2,1,0:T(8,128)(2,1)}, u32[]{:S(2)}, u32[]{:S(2)}) async-start(bf16[16,128,384]{2,1,0:T(8,128)(2,1)} %param.13), calls=%async_computation.1 | async-start | bytes 3145728 | tf_op jit(solution)/shard_map/all_to_all | solution.py:120
  109.2 136.2 %all-gather.2.cloned.1.call-start = ((), (), s32[]{:S(2)}) async-start(), calls=%async_computation.6 | async-start | bytes 8650752 | tf_op jit(solution)/shard_map/all_gather | solution.py:107
  151.9 217.4 %all-to-all-start = ((bf16[32,64,2048]{2,1,0:T(8,128)(2,1)}), bf16[32,64,2048]{2,1,0:T(8,128)(2,1)}, u32[]{:S(2)}, u32[]{:S(2)}) async-start(bf16[32,64,2048]{2,1,0:T(8,128)(2,1)} %stack.2), calls=%async_computation | async-start | bytes 16777216 | tf_op jit(solution)/shard_map/all_to_all | solution.py:111
  161.5 385.9 %reduce-scatter.2.cloned.1.call-start = ((), (), s32[]{:S(2)}) async-start(), calls=%async_computation.7 | async-start | bytes 8650752 | tf_op jit(solution)/shard_map/reduce_scatter | solution.py:134
  245.3 10.1 %copy-start.8 = (bf16[2048,2048]{1,0:T(8,128)(2,1)S(1)}, bf16[2048,2048]{1,0:T(8,128)(2,1)}, u32[]{:S(2)}) copy-start(bf16[2048,2048]{1,0:T(8,128)(2,1)} %all-gather.2.cloned.1.call-done) | copy-start | bytes 25165828
  369.3 11.6 %copy-start.2 = (bf16[16,128,384]{2,1,0:T(8,128)(2,1)S(1)}, bf16[16,128,384]{2,1,0:T(8,128)(2,1)}, u32[]{:S(2)}) copy-start(bf16[16,128,384]{2,1,0:T(8,128)(2,1)} %all_to_all.42) | copy-start | bytes 4718596
  380.9 8.3 %copy-start.5 = (bf16[2048,384]{1,0:T(8,128)(2,1)}, bf16[2048,384]{1,0:T(8,128)(2,1)S(1)}, u32[]{:S(2)}) copy-start(bf16[2048,384]{1,0:T(8,128)(2,1)S(1)} %get-tuple-element.5) | copy-start | bytes 4718596
  380.9 8.3 %copy-start.3 = (bf16[2048,384]{1,0:T(8,128)(2,1)}, bf16[2048,384]{1,0:T(8,128)(2,1)S(1)}, u32[]{:S(2)}) copy-start(bf16[2048,384]{1,0:T(8,128)(2,1)S(1)} %get-tuple-element.4) | copy-start | bytes 4718596
  399.5 9.7 %copy-start.4 = (bf16[2048,384]{1,0:T(8,128)(2,1)S(1)}, bf16[2048,384]{1,0:T(8,128)(2,1)}, u32[]{:S(2)}) copy-start(bf16[2048,384]{1,0:T(8,128)(2,1)} %copy-done.3) | copy-start | bytes 4718596
  409.2 9.3 %copy-start.9 = (f32[2048,384]{1,0:T(8,128)S(1)}, f32[2048,384]{1,0:T(8,128)}, u32[]{:S(2)}) copy-start(f32[2048,384]{1,0:T(8,128)} %fusion.7) | copy-start | bytes 9437188
  409.2 9.3 %copy-start.10 = (f32[2048,384]{1,0:T(8,128)S(1)}, f32[2048,384]{1,0:T(8,128)}, u32[]{:S(2)}) copy-start(f32[2048,384]{1,0:T(8,128)} %fusion.6) | copy-start | bytes 9437188
  418.5 132.1 %copy-start.1 = (bf16[128,2048]{1,0:T(8,128)(2,1)S(1)}, bf16[128,2048]{1,0:T(8,128)(2,1)}, u32[]{:S(2)}) copy-start(bf16[128,2048]{1,0:T(8,128)(2,1)} %param.7) | copy-start | bytes 1572868
Sparse Core Ops, SparseCore 0:
  113.4 131.8 all-gather.1
  399.6 147.7 reduce-scatter.1
